TPU v7x, 256 devices: a whole 4x4x8 slice. The times are simulated.
256 devices in a mesh: row: 8 (over z_hi, x), col: 32 (over y, z_lo, core).
Axes of the slice: x: 4, y: 4, z: 8 (z_hi: 2, z_lo: 4; z = z_hi * 4 + z_lo), core: 2. Of those that a mesh axis runs over, the one named last changes fastest.
Arguments:
- prior_cov: float32 [16384, 16384], P('row', 'col'), as said below
- diffusivity: float32 [16384], replicated, may hold values from 0.05 to 0.2
- velocity: float32 [2, 16384], replicated, may hold values from -0.3 to 0.3
- process_noise_variance: float32 [16384], replicated, may hold values from 0.2 to 1
- observed_index: int32 [256], replicated, may hold values from 0 to 16383, as said below
- innov_factor: float32 [256, 256], replicated, may hold values from -0.048 to 1.048
Outputs:
- analysis_cov: float32 [16384, 16384], P('row', 'col')
Inputs may be any that keep to these rules, and one draw needn't show every extreme that they name: `prior_cov`: symmetric positive definite. `observed_index`: 256 distinct point indices.
All inputs are finite; a program needn't handle non-finite values.
Results may differ from a plain program's by a relative error of at most 0.000098.
Values sent between devices are 32-bit elements; how exact they have to be, the bound alone decides.
A program may use at most 128 MiB of HBM per device.

v0:
```python
import jax
import jax.numpy as jnp
from jax import lax
from jax.sharding import PartitionSpec as P

GY = 128
STEPS = 2


def with_halo(shard, sides, width):
    for axis, dim in sides:
        peers, length = (lax.axis_size(axis), shard.shape[dim])
        up = [(i, (i + 1) % peers) for i in range(peers - 1)]
        down = [(j, i) for i, j in up]
        last = lax.slice_in_dim(shard, length - width, length, axis=dim)
        leading = lax.slice_in_dim(shard, 0, width, axis=dim)
        before = lax.ppermute(last, axis, up)
        after = lax.ppermute(leading, axis, down)
        shard = jnp.concatenate([before, shard, after], axis=dim)
    return shard


def advect(values, diffuse_coef, east_speed, south_speed, grid_axis):
    extent = values.shape[grid_axis]
    north_side = lax.slice_in_dim(values, 0, extent - 2, axis=grid_axis)
    center = lax.slice_in_dim(values, 1, extent - 1, axis=grid_axis)
    south_side = lax.slice_in_dim(values, 2, extent, axis=grid_axis)
    span_cols = values.shape[grid_axis + 1]
    zero_edge = jnp.zeros_like(lax.slice_in_dim(center, 0, 1, axis=grid_axis + 1))
    east_side = jnp.concatenate(
        [lax.slice_in_dim(center, 1, span_cols, axis=grid_axis + 1), zero_edge], axis=grid_axis + 1
    )
    west_side = jnp.concatenate(
        [zero_edge, lax.slice_in_dim(center, 0, span_cols - 1, axis=grid_axis + 1)],
        axis=grid_axis + 1,
    )
    laplace = north_side + south_side + east_side + west_side - 4.0 * center
    return (
        center
        + diffuse_coef * laplace
        - 0.5 * east_speed * (east_side - west_side)
        - 0.5 * south_speed * (south_side - north_side)
    )


def on_device(
    prior_cov, diffusivity, velocity, process_noise_variance, observed_index, innov_factor
):
    top_precision = lax.Precision.HIGHEST
    rows_dev, cols_dev = prior_cov.shape
    row_start = lax.axis_index("row") * rows_dev
    col_start = lax.axis_index("col") * cols_dev
    margin = GY * STEPS
    diffuse_pad = jnp.pad(diffusivity, (margin, margin))
    east_pad = jnp.pad(velocity[0], (margin, margin))
    south_pad = jnp.pad(velocity[1], (margin, margin))

    def window(offset, amount, shaped):
        return tuple(
            (
                lax.dynamic_slice_in_dim(table, offset + margin, amount).reshape(shaped)
                for table in (diffuse_pad, east_pad, south_pad)
            )
        )

    present_state = prior_cov
    coefs = window(row_start, rows_dev, (rows_dev // GY, GY, 1))
    for substep in range(STEPS):
        widened = with_halo(present_state, (("row", 0),), GY)
        present_state = advect(
            widened.reshape(-1, GY, cols_dev), coefs[0], coefs[1], coefs[2], 0
        ).reshape(rows_dev, cols_dev)
    coefs = window(col_start, cols_dev, (1, cols_dev // GY, GY))
    for substep in range(STEPS):
        widened = with_halo(present_state, (("col", 1),), GY)
        present_state = advect(
            widened.reshape(rows_dev, -1, GY), coefs[0], coefs[1], coefs[2], 1
        ).reshape(rows_dev, cols_dev)
    row_labels = row_start + lax.iota(jnp.int32, rows_dev)
    column_labels = col_start + lax.iota(jnp.int32, cols_dev)
    variance_rows = lax.dynamic_slice_in_dim(process_noise_variance, row_start, rows_dev)
    predicted_cov = present_state + jnp.where(
        row_labels[:, None] == column_labels[None, :], variance_rows[:, None], 0.0
    )
    pick_cols = (column_labels[:, None] == observed_index[None, :]).astype(jnp.float32)
    pick_rows = (row_labels[:, None] == observed_index[None, :]).astype(jnp.float32)
    stencil_weights = jnp.dot(
        pick_cols, innov_factor.T, precision=top_precision, preferred_element_type=jnp.float32
    )
    partial_left_product = jnp.dot(
        predicted_cov, stencil_weights, precision=top_precision, preferred_element_type=jnp.float32
    )
    left_multiplier = lax.psum(partial_left_product, "col")
    observed = lax.dot_general(
        pick_rows,
        predicted_cov,
        (((0,), (0,)), ((), ())),
        precision=top_precision,
        preferred_element_type=jnp.float32,
    )
    observed = lax.psum(observed, "row")
    right_multiplier = jnp.dot(
        innov_factor, observed, precision=top_precision, preferred_element_type=jnp.float32
    )
    return predicted_cov - jnp.dot(
        left_multiplier,
        right_multiplier,
        precision=top_precision,
        preferred_element_type=jnp.float32,
    )


def solution(mesh):
    return jax.shard_map(
        on_device,
        mesh=mesh,
        in_specs=(P("row", "col"), P(), P(), P(), P(), P()),
        out_specs=P("row", "col"),
        check_vma=False,
    )
```

profile of v0, /device:TPU:1, one launch (start us, length us, event | category | flops | bytes accessed | tf_op | source)
XLA Modules:
  0.0 592.9 jit_solution(15418751431844451939)
XLA Ops:
  6.5 1.1 fusion.40
  7.6 3.9 collective-permute-start
  11.6 1.3 collective-permute-start.1
  12.9 1.1 fusion.41
  14.0 5.4 copy.11
  19.4 7.9 %fusion.39 = (f32[16,127,512]{1,0,2:T(8,128)}, f32[16,127,512]{1,0,2:T(8,128)}) fusion(f32[16,128,512]{1,0,2:T(8,128)} %copy.11), kind=kLoop, calls=%fused_computation.66 | loop fusion | bytes 16646144 | tf_op jit(solution)/shard_map/slice | solution.py:31
  27.5 7.7 %fusion.6 = (f32[2048,512]{1,0:T(8,128)}, f32[2048,512]{1,0:T(8,128)}) fusion(f32[2048,512]{1,0:T(8,128)} %param.6, f32[128,512]{1,0:T(8,128)S(1)} %collective-permute-done, f32[128,512]{1,0:T(8,128)S(1)} %collective-permute-done.1), kind=kLoop, calls=%fused_computation.22 | loop fusion | flops 4194304 | bytes 13107200 | tf_op jit(solution)/shard_map/add | solution.py:37
  35.2 5.4 copy.12
  40.6 5.4 copy.8
  46.1 8.1 %multiply_subtract_fusion.2 = f32[16,128,512]{1,0,2:T(8,128)S(1)} fusion(f32[16,128,512]{1,0,2:T(8,128)} %copy.12, f32[16,128,512]{1,0,2:T(8,128)} %copy.11, f32[16,127,512]{1,0,2:T(8,128)} %get-tuple-element.22, f32[16,128,512]{1,0,2:T(8,128)} %copy.8, f32[16,127,512]{1,0,2:T(8,128)} %get-tuple-element.21, f32[16,128]{1,0:T(8,128)S(1)} %fusion.29, ...), kind=kLoop, calls=%fused_computation.21 | loop fusion | flops 11534336 | bytes 25124864 | tf_op jit(solution)/shard_map/sub | solution.py:39
  54.5 4.0 collective-permute-start.2
  58.5 1.5 collective-permute-start.3
  60.0 3.4 fusion.37
  63.4 2.0 copy.22
  65.3 1.4 collective-permute-done.3
  66.7 1.1 add_bitcast_fusion
  67.9 0.9 copy.16
  68.8 0.9 copy.17
  69.8 1.2 copy-done.3
  71.0 2.7 fusion
  73.7 2.0 copy.21
  75.7 2.0 copy-done.1
  77.7 1.2 fusion.36
  78.9 5.8 collective-permute-start.4
  84.7 2.1 collective-permute-start.5
  86.9 0.8 fusion.30
  87.7 13.6 %collective-permute-done.4 = f32[2048,128]{0,1:T(8,128)S(1)} collective-permute-done((f32[2048,128]{0,1:T(8,128)}, f32[2048,128]{0,1:T(8,128)S(1)}, u32[]{:S(2)}, u32[]{:S(2)}) %collective-permute-start.4) | collective-permute-done | bytes 1048608 | tf_op jit(solution)/shard_map/ppermute | solution.py:17
  101.4 8.0 %collective-permute-done.5 = f32[2048,128]{0,1:T(8,128)S(1)} collective-permute-done((f32[2048,128]{0,1:T(8,128)S(1)}, f32[2048,128]{0,1:T(8,128)S(1)}, u32[]{:S(2)}, u32[]{:S(2)}) %collective-permute-start.5) | collective-permute-done | bytes 1048608 | tf_op jit(solution)/shard_map/ppermute | solution.py:18
  109.4 2.6 pad_maximum_fusion
  112.0 1.2 fusion.34
  113.2 2.7 multiply_subtract_fusion.1
  115.9 2.0 copy-done.2
  117.9 1.2 fusion.35
  119.1 1.9 collective-permute-start.6
  121.0 2.5 collective-permute-start.7
  123.5 0.7 dynamic_slice.27
  124.2 8.8 %collective-permute-done.6 = f32[2048,128]{0,1:T(8,128)S(1)} collective-permute-done((f32[2048,128]{0,1:T(8,128)}, f32[2048,128]{0,1:T(8,128)S(1)}, u32[]{:S(2)}, u32[]{:S(2)}) %collective-permute-start.6) | collective-permute-done | bytes 1048608 | tf_op jit(solution)/shard_map/ppermute | solution.py:17
  133.1 17.9 %collective-permute-done.7 = f32[2048,128]{0,1:T(8,128)S(1)} collective-permute-done((f32[2048,128]{0,1:T(8,128)S(1)}, f32[2048,128]{0,1:T(8,128)S(1)}, u32[]{:S(2)}, u32[]{:S(2)}) %collective-permute-start.7) | collective-permute-done | bytes 1048608 | tf_op jit(solution)/shard_map/ppermute | solution.py:18
  151.0 2.6 pad_maximum_fusion.1
  153.6 1.2 fusion.33
  154.8 4.1 multiply_subtract_fusion
  159.0 5.3 copy.14
  164.3 6.1 %fusion.8 = f32[256,512]{1,0:T(8,128)} fusion(f32[2048,512]{1,0:T(8,128)} %copy.14, f32[2048]{0:T(1024)S(1)} %dynamic_slice.27, s32[512]{0:T(512)S(1)} %iota_add_fusion.1, s32[2048]{0:T(1024)S(1)} %iota_add_fusion, s32[256]{0:T(256)S(1)} %copy-done.5), kind=kOutput, calls=%fused_computation.25 | convolution fusion | flops 3224895488 | bytes 4738048 | tf_op jit(solution)/shard_map/dot_general | solution.py:94
  171.2 7.2 %fusion.9 = f32[2048,256]{1,0:T(8,128)} fusion(f32[512,256]{1,0:T(8,128)S(1)} %fusion.21, f32[2048,512]{1,0:T(8,128)} %copy.14, f32[2048]{0:T(1024)S(1)} %dynamic_slice.27, s32[512]{0:T(512)S(1)} %iota_add_fusion.1, s32[2048]{0:T(1024)S(1)} %iota_add_fusion), kind=kOutput, calls=%fused_computation.26 | convolution fusion | flops 3224371200 | bytes 6834176 | tf_op jit(solution)/shard_map/dot_general | solution.py:90
  178.4 111.9 %all-reduce.16.cloned.1.call-done = f32[256,512]{1,0:T(8,128)} async-done(((f32[256,512]{1,0:T(8,128)}), f32[256,512]{1,0:T(8,128)}) %all-reduce.16.cloned.1.call-update) | async-done | bytes 524304 | tf_op jit(solution)/shard_map/psum | solution.py:101
  290.3 2.0 fusion.42
  292.4 285.0 %all-reduce.14.cloned.1.call-done = f32[2048,256]{1,0:T(8,128)} async-done(((f32[2048,256]{1,0:T(8,128)}), f32[2048,256]{1,0:T(8,128)}) %all-reduce.14.cloned.1.call-update) | async-done | bytes 2097168 | tf_op jit(solution)/shard_map/psum | solution.py:93
  577.4 8.7 %convolution_subtract_fusion = f32[2048,512]{1,0:T(8,128)} fusion(f32[2048,256]{1,0:T(8,128)} %all-reduce.14.cloned.1.call-done, f32[512,256]{1,0:T(8,128)S(1)} %fusion.42, f32[2048,512]{1,0:T(8,128)} %copy.14, f32[2048]{0:T(1024)S(1)} %dynamic_slice.27, s32[512]{0:T(512)S(1)} %iota_add_fusion.1, s32[2048]{0:T(1024)S(1)} %iota_add_fusion), kind=kOutput, calls=%fused_computation.24 | convolution fusion | flops 3225419776 | bytes 11028480 | tf_op jit(solution)/shard_map/dot_general | solution.py:105
  (23 shorter events, 1.4 us)
Async XLA Ops:
  6.5 164.2 %copy-start = (f32[256,256]{1,0:T(8,128)S(1)}, f32[256,256]{1,0:T(8,128)}, u32[]{:S(2)}) copy-start(f32[256,256]{1,0:T(8,128)} %param.11) | copy-start | bytes 786436
  6.5 283.8 %all-reduce.16.cloned.1.call-start = ((), (), s32[]{:S(2)}) async-start(), calls=%async_computation.1 | async-start | bytes 1048576 | tf_op jit(solution)/shard_map/psum | solution.py:101
  7.6 19.9 %collective-permute-start = (f32[128,512]{1,0:T(8,128)S(1)}, f32[128,512]{1,0:T(8,128)S(1)}, u32[]{:S(2)}, u32[]{:S(2)}) collective-permute-start(f32[128,512]{1,0:T(8,128)S(1)} %get-tuple-element.24), channel_id=1, source_target_pairs={{0,32},{32,64},{64,96},{96,128},{128,160},{160,192},{192,224},{1,3... | collective-permute-start | bytes 786440 | tf_op jit(solution)/shard_map/ppermute | solution.py:17
  11.6 15.9 %collective-permute-start.1 = (f32[128,512]{1,0:T(8,128)S(1)}, f32[128,512]{1,0:T(8,128)S(1)}, u32[]{:S(2)}, u32[]{:S(2)}) collective-permute-start(f32[128,512]{1,0:T(8,128)S(1)} %get-tuple-element.23), channel_id=1, source_target_pairs={{32,0},{64,32},{96,64},{128,96},{160,128},{192,160},{224,192},{33,... | collective-permute-start | bytes 786440 | tf_op jit(solution)/shard_map/ppermute | solution.py:18
  19.4 8.0 %copy-start.4 = (f32[16384]{0:T(1024)S(1)}, f32[16384]{0:T(1024)}, u32[]{:S(2)}) copy-start(f32[16384]{0:T(1024)} %param.7) | copy-start | bytes 196612
  54.5 10.8 %collective-permute-start.2 = (f32[128,512]{0,1:T(8,128)S(1)}, f32[128,512]{0,1:T(8,128)S(1)}, u32[]{:S(2)}, u32[]{:S(2)}) collective-permute-start(f32[128,512]{0,1:T(8,128)S(1)} %bitcast.87), channel_id=1, source_target_pairs={{0,32},{32,64},{64,96},{96,128},{128,160},{160,192},{192,224},{1,3... | collective-permute-start | bytes 786440 | tf_op jit(solution)/shard_map/ppermute | solution.py:17
  58.5 8.2 %collective-permute-start.3 = (f32[128,512]{0,1:T(8,128)S(1)}, f32[128,512]{0,1:T(8,128)S(1)}, u32[]{:S(2)}, u32[]{:S(2)}) collective-permute-start(f32[128,512]{0,1:T(8,128)S(1)} %bitcast.86), channel_id=1, source_target_pairs={{32,0},{64,32},{96,64},{128,96},{160,128},{192,160},{224,192},{33,... | collective-permute-start | bytes 786440 | tf_op jit(solution)/shard_map/ppermute | solution.py:18
  68.8 2.2 copy-start.3
  75.7 2.0 copy-start.1
  78.9 22.5 %collective-permute-start.4 = (f32[2048,128]{0,1:T(8,128)}, f32[2048,128]{0,1:T(8,128)S(1)}, u32[]{:S(2)}, u32[]{:S(2)}) collective-permute-start(f32[2048,128]{0,1:T(8,128)} %get-tuple-element.15), channel_id=1, source_target_pairs={{0,1},{1,2},{2,3},{3,4},{4,5},{5,6},{6,7},{7,8},{8,9},{9,10},{10,1... | collective-permute-start | bytes 3145736 | tf_op jit(solution)/shard_map/ppermute | solution.py:17
  84.7 24.6 %collective-permute-start.5 = (f32[2048,128]{0,1:T(8,128)S(1)}, f32[2048,128]{0,1:T(8,128)S(1)}, u32[]{:S(2)}, u32[]{:S(2)}) collective-permute-start(f32[2048,128]{0,1:T(8,128)S(1)} %get-tuple-element.16), channel_id=1, source_target_pairs={{1,0},{2,1},{3,2},{4,3},{5,4},{6,5},{7,6},{8,7},{9,8},{10,9},{11,1... | collective-permute-start | bytes 3145736 | tf_op jit(solution)/shard_map/ppermute | solution.py:18
  115.9 2.0 copy-start.2
  119.1 14.0 %collective-permute-start.6 = (f32[2048,128]{0,1:T(8,128)}, f32[2048,128]{0,1:T(8,128)S(1)}, u32[]{:S(2)}, u32[]{:S(2)}) collective-permute-start(f32[2048,128]{0,1:T(8,128)} %get-tuple-element.13), channel_id=1, source_target_pairs={{0,1},{1,2},{2,3},{3,4},{4,5},{5,6},{6,7},{7,8},{8,9},{9,10},{10,1... | collective-permute-start | bytes 3145736 | tf_op jit(solution)/shard_map/ppermute | solution.py:17
  121.0 30.0 %collective-permute-start.7 = (f32[2048,128]{0,1:T(8,128)S(1)}, f32[2048,128]{0,1:T(8,128)S(1)}, u32[]{:S(2)}, u32[]{:S(2)}) collective-permute-start(f32[2048,128]{0,1:T(8,128)S(1)} %get-tuple-element.14), channel_id=1, source_target_pairs={{1,0},{2,1},{3,2},{4,3},{5,4},{6,5},{7,6},{8,7},{9,8},{10,9},{11,1... | collective-permute-start | bytes 3145736 | tf_op jit(solution)/shard_map/ppermute | solution.py:18
  159.0 5.3 copy-start.5
  170.4 406.9 %all-reduce.14.cloned.1.call-start = ((), (), s32[]{:S(2)}) async-start(), calls=%async_computation | async-start | bytes 4194304 | tf_op jit(solution)/shard_map/psum | solution.py:93
Sparse Core Ops, SparseCore 0:
  170.6 119.7 all-reduce.15
  292.9 284.3 all-reduce.13
where the time goes:
time: 594 us; the launch traced here: 593 us
  waiting for transfers between devices  447 us (75%)
  local copies, waits for them, and re-layouts  52.8 us (9%)
  other arithmetic  31.9 us (5%)
  matrix products  24.5 us (4%)
  starting transfers between devices  23.3 us (4%)
  between operations  13.6 us (2%)
    psum x1, waiting for transfers between devices, on_device(): left_multiplier = lax.psum(partial_left_product, 'col')  285 us
    psum x1, waiting for transfers between devices, on_device(): observed = lax.psum(observed, 'row')  112 us
    ppermute x4, waiting for transfers between devices, with_halo(): after = lax.ppermute(leading, axis, down)  27.3 us
    ppermute x4, waiting for transfers between devices, with_halo(): before = lax.ppermute(last, axis, up)  22.5 us
    sub x4, other arithmetic, advect(): center + diffuse_coef * laplace - 0.5 * east_speed * (east_side - west_side)  17.6 us
    ppermute x4, starting transfers between devices, with_halo(): before = lax.ppermute(last, axis, up)  15.7 us
    slice x4, local copies, waits for them, and re-layouts, advect(): lax.slice_in_dim(center, 1, span_cols, axis=grid_axis + 1)  13.7 us
  transfers between devices with their start and end apart: 10, of which 7 were waited for; matrix products, arithmetic and copies ran while one was open for 5% of the time, Pallas kernels for 0%

commit v1 on v0

--- a/solution.py
+++ b/solution.py
@@ -98,7 +98,8 @@
         precision=top_precision,
         preferred_element_type=jnp.float32,
     )
-    observed = lax.psum(observed, "row")
+    shards = lax.all_gather(observed, "row", axis=0, tiled=False)
+    observed = shards.sum(axis=0)
     right_multiplier = jnp.dot(
         innov_factor, observed, precision=top_precision, preferred_element_type=jnp.float32
     )

time: 594 us -> 545 us (0.918)
  waiting for transfers between devices: 447 us -> 395 us
    psum x1 -> x0, waiting for transfers between devices: 112 us -> none  [on_device(): observed = lax.psum(observed, 'row')]
    all_gather x0 -> x1, waiting for transfers between devices: none -> 101 us  [on_device(): shards = lax.all_gather(observed, 'row', axis=0, tiled=False)]
    psum x1, waiting for transfers between devices: 285 us -> 244 us  [on_device(): left_multiplier = lax.psum(partial_left_product, 'col')]
  transfers between devices with their start and end apart: 10 -> 10, of which waited for: 7 -> 7; matrix products, arithmetic and copies ran while one was open for 5% -> 6% of each run, Pallas kernels for 0% -> 0%
where the time goes in v1:
time: 545 us; the launch traced here: 544 us
  waiting for transfers between devices  395 us (72%)
  local copies, waits for them, and re-layouts  52.8 us (10%)
  other arithmetic  34.6 us (6%)
  matrix products  23.4 us (4%)
  starting transfers between devices  23.3 us (4%)
  between operations  15.1 us (3%)
    psum x1, waiting for transfers between devices, on_device(): left_multiplier = lax.psum(partial_left_product, 'col')  244 us
    all_gather x1, waiting for transfers between devices, on_device(): shards = lax.all_gather(observed, 'row', axis=0, tiled=False)  101 us
    ppermute x4, waiting for transfers between devices, with_halo(): after = lax.ppermute(leading, axis, down)  27.3 us
    ppermute x4, waiting for transfers between devices, with_halo(): before = lax.ppermute(last, axis, up)  22.5 us
    sub x4, other arithmetic, advect(): center + diffuse_coef * laplace - 0.5 * east_speed * (east_side - west_side)  17.6 us
    ppermute x4, starting transfers between devices, with_halo(): before = lax.ppermute(last, axis, up)  15.7 us
    slice x4, local copies, waits for them, and re-layouts, advect(): lax.slice_in_dim(center, 1, span_cols, axis=grid_axis + 1)  13.7 us
    unnamed x16, local copies, waits for them, and re-layouts  11 us
  transfers between devices with their start and end apart: 10, of which 7 were waited for; matrix products, arithmetic and copies ran while one was open for 6% of the time, Pallas kernels for 0%

profile of v1, /device:TPU:1, one launch (start us, length us, event | category | flops | bytes accessed | tf_op | source)
XLA Modules:
  0.0 544.3 jit_solution(3032923433871870497)
XLA Ops:
  7.4 1.1 fusion.40
  8.5 3.9 collective-permute-start
  12.4 1.3 collective-permute-start.1
  13.7 1.1 fusion.41
  14.8 5.4 copy.11
  20.3 7.9 %fusion.39 = (f32[16,127,512]{1,0,2:T(8,128)}, f32[16,127,512]{1,0,2:T(8,128)}) fusion(f32[16,128,512]{1,0,2:T(8,128)} %copy.11), kind=kLoop, calls=%fused_computation.66 | loop fusion | bytes 16646144 | tf_op jit(solution)/shard_map/slice | solution.py:31
  28.3 7.7 %fusion.6 = (f32[2048,512]{1,0:T(8,128)}, f32[2048,512]{1,0:T(8,128)}) fusion(f32[2048,512]{1,0:T(8,128)} %param.6, f32[128,512]{1,0:T(8,128)S(1)} %collective-permute-done, f32[128,512]{1,0:T(8,128)S(1)} %collective-permute-done.1), kind=kLoop, calls=%fused_computation.22 | loop fusion | flops 4194304 | bytes 13107200 | tf_op jit(solution)/shard_map/add | solution.py:37
  36.0 5.4 copy.12
  41.5 5.4 copy.8
  46.9 8.1 %multiply_subtract_fusion.2 = f32[16,128,512]{1,0,2:T(8,128)S(1)} fusion(f32[16,128,512]{1,0,2:T(8,128)} %copy.12, f32[16,128,512]{1,0,2:T(8,128)} %copy.11, f32[16,127,512]{1,0,2:T(8,128)} %get-tuple-element.22, f32[16,128,512]{1,0,2:T(8,128)} %copy.8, f32[16,127,512]{1,0,2:T(8,128)} %get-tuple-element.21, f32[16,128]{1,0:T(8,128)S(1)} %fusion.29, ...), kind=kLoop, calls=%fused_computation.21 | loop fusion | flops 11534336 | bytes 25124864 | tf_op jit(solution)/shard_map/sub | solution.py:39
  55.3 4.0 collective-permute-start.2
  59.3 1.5 collective-permute-start.3
  60.8 3.4 fusion.37
  64.2 2.0 copy.22
  66.2 1.4 collective-permute-done.3
  67.6 1.1 add_bitcast_fusion
  68.7 0.9 copy.16
  69.7 0.9 copy.17
  70.6 1.2 copy-done.3
  71.8 2.7 fusion
  74.6 2.0 copy.21
  76.5 2.0 copy-done.1
  78.6 1.2 fusion.36
  79.8 5.8 %collective-permute-start.4 = (f32[2048,128]{0,1:T(8,128)}, f32[2048,128]{0,1:T(8,128)S(1)}, u32[]{:S(2)}, u32[]{:S(2)}) collective-permute-start(f32[2048,128]{0,1:T(8,128)} %get-tuple-element.15), channel_id=1, source_target_pairs={{0,1},{1,2},{2,3},{3,4},{4,5},{5,6},{6,7},{7,8},{8,9},{9,10},{10,1... | collective-permute-start | bytes 3145736 | tf_op jit(solution)/shard_map/ppermute | solution.py:17
  85.6 2.1 collective-permute-start.5
  87.7 0.8 fusion.30
  88.6 13.6 %collective-permute-done.4 = f32[2048,128]{0,1:T(8,128)S(1)} collective-permute-done((f32[2048,128]{0,1:T(8,128)}, f32[2048,128]{0,1:T(8,128)S(1)}, u32[]{:S(2)}, u32[]{:S(2)}) %collective-permute-start.4) | collective-permute-done | bytes 1048608 | tf_op jit(solution)/shard_map/ppermute | solution.py:17
  102.2 8.0 %collective-permute-done.5 = f32[2048,128]{0,1:T(8,128)S(1)} collective-permute-done((f32[2048,128]{0,1:T(8,128)S(1)}, f32[2048,128]{0,1:T(8,128)S(1)}, u32[]{:S(2)}, u32[]{:S(2)}) %collective-permute-start.5) | collective-permute-done | bytes 1048608 | tf_op jit(solution)/shard_map/ppermute | solution.py:18
  110.2 2.6 pad_maximum_fusion
  112.8 1.2 fusion.34
  114.0 2.7 multiply_subtract_fusion.1
  116.8 2.0 copy-done.2
  118.8 1.2 fusion.35
  120.0 1.9 collective-permute-start.6
  121.9 2.5 collective-permute-start.7
  125.1 8.8 %collective-permute-done.6 = f32[2048,128]{0,1:T(8,128)S(1)} collective-permute-done((f32[2048,128]{0,1:T(8,128)}, f32[2048,128]{0,1:T(8,128)S(1)}, u32[]{:S(2)}, u32[]{:S(2)}) %collective-permute-start.6) | collective-permute-done | bytes 1048608 | tf_op jit(solution)/shard_map/ppermute | solution.py:17
  133.9 17.9 %collective-permute-done.7 = f32[2048,128]{0,1:T(8,128)S(1)} collective-permute-done((f32[2048,128]{0,1:T(8,128)S(1)}, f32[2048,128]{0,1:T(8,128)S(1)}, u32[]{:S(2)}, u32[]{:S(2)}) %collective-permute-start.7) | collective-permute-done | bytes 1048608 | tf_op jit(solution)/shard_map/ppermute | solution.py:18
  151.8 2.6 pad_maximum_fusion.1
  154.5 1.2 fusion.33
  155.7 4.1 multiply_subtract_fusion
  159.8 5.3 copy.14
  165.1 6.1 %fusion.8 = f32[256,512]{1,0:T(8,128)} fusion(f32[2048,512]{1,0:T(8,128)} %copy.14, f32[2048]{0:T(1024)S(1)} %dynamic_slice.27, s32[512]{0:T(512)S(1)} %iota_add_fusion.1, s32[2048]{0:T(1024)S(1)} %iota_add_fusion, s32[256]{0:T(256)S(1)} %copy-done.5), kind=kOutput, calls=%fused_computation.25 | convolution fusion | flops 3224895488 | bytes 4738048 | tf_op jit(solution)/shard_map/dot_general | solution.py:94
  172.0 7.2 %fusion.9 = f32[2048,256]{1,0:T(8,128)} fusion(f32[512,256]{1,0:T(8,128)S(1)} %fusion.21, f32[2048,512]{1,0:T(8,128)} %copy.14, f32[2048]{0:T(1024)S(1)} %dynamic_slice.27, s32[512]{0:T(512)S(1)} %iota_add_fusion.1, s32[2048]{0:T(1024)S(1)} %iota_add_fusion), kind=kOutput, calls=%fused_computation.26 | convolution fusion | flops 3224371200 | bytes 6834176 | tf_op jit(solution)/shard_map/dot_general | solution.py:90
  179.3 101.2 %all-gather.3.cloned.1.call-done = f32[2048,512]{1,0:T(8,128)} async-done(((f32[256,512]{1,0:T(8,128)}), f32[2048,512]{1,0:T(8,128)}) %all-gather.3.cloned.1.call-update) | async-done | bytes 4194320 | tf_op jit(solution)/shard_map/all_gather | solution.py:101
  280.4 2.7 reduce_sum.9
  283.2 1.0 fusion.42
  284.2 244.0 %all-reduce.13.cloned.1.call-done = f32[2048,256]{1,0:T(8,128)} async-done(((f32[2048,256]{1,0:T(8,128)}), f32[2048,256]{1,0:T(8,128)}) %all-reduce.13.cloned.1.call-update) | async-done | bytes 2097168 | tf_op jit(solution)/shard_map/psum | solution.py:93
  528.2 8.7 %convolution_subtract_fusion = f32[2048,512]{1,0:T(8,128)} fusion(f32[2048,256]{1,0:T(8,128)} %all-reduce.13.cloned.1.call-done, f32[512,256]{1,0:T(8,128)S(1)} %fusion.42, f32[2048,512]{1,0:T(8,128)} %copy.14, f32[2048]{0:T(1024)S(1)} %dynamic_slice.27, s32[512]{0:T(512)S(1)} %iota_add_fusion.1, s32[2048]{0:T(1024)S(1)} %iota_add_fusion), kind=kOutput, calls=%fused_computation.24 | convolution fusion | flops 3225419776 | bytes 11028480 | tf_op jit(solution)/shard_map/dot_general | solution.py:106
  (24 shorter events, 2.1 us)
Async XLA Ops:
  7.4 164.2 %copy-start = (f32[256,256]{1,0:T(8,128)S(1)}, f32[256,256]{1,0:T(8,128)}, u32[]{:S(2)}) copy-start(f32[256,256]{1,0:T(8,128)} %param.11) | copy-start | bytes 786436
  7.4 273.1 %all-gather.3.cloned.1.call-start = ((), (), s32[]{:S(2)}) async-start(), calls=%async_computation.1 | async-start | bytes 4718592 | tf_op jit(solution)/shard_map/all_gather | solution.py:101
  8.5 19.9 %collective-permute-start = (f32[128,512]{1,0:T(8,128)S(1)}, f32[128,512]{1,0:T(8,128)S(1)}, u32[]{:S(2)}, u32[]{:S(2)}) collective-permute-start(f32[128,512]{1,0:T(8,128)S(1)} %get-tuple-element.24), channel_id=1, source_target_pairs={{0,32},{32,64},{64,96},{96,128},{128,160},{160,192},{192,224},{1,3... | collective-permute-start | bytes 786440 | tf_op jit(solution)/shard_map/ppermute | solution.py:17
  12.4 15.9 %collective-permute-start.1 = (f32[128,512]{1,0:T(8,128)S(1)}, f32[128,512]{1,0:T(8,128)S(1)}, u32[]{:S(2)}, u32[]{:S(2)}) collective-permute-start(f32[128,512]{1,0:T(8,128)S(1)} %get-tuple-element.23), channel_id=1, source_target_pairs={{32,0},{64,32},{96,64},{128,96},{160,128},{192,160},{224,192},{33,... | collective-permute-start | bytes 786440 | tf_op jit(solution)/shard_map/ppermute | solution.py:18
  20.3 8.0 %copy-start.4 = (f32[16384]{0:T(1024)S(1)}, f32[16384]{0:T(1024)}, u32[]{:S(2)}) copy-start(f32[16384]{0:T(1024)} %param.7) | copy-start | bytes 196612
  55.3 10.8 %collective-permute-start.2 = (f32[128,512]{0,1:T(8,128)S(1)}, f32[128,512]{0,1:T(8,128)S(1)}, u32[]{:S(2)}, u32[]{:S(2)}) collective-permute-start(f32[128,512]{0,1:T(8,128)S(1)} %bitcast.89), channel_id=1, source_target_pairs={{0,32},{32,64},{64,96},{96,128},{128,160},{160,192},{192,224},{1,3... | collective-permute-start | bytes 786440 | tf_op jit(solution)/shard_map/ppermute | solution.py:17
  59.3 8.2 %collective-permute-start.3 = (f32[128,512]{0,1:T(8,128)S(1)}, f32[128,512]{0,1:T(8,128)S(1)}, u32[]{:S(2)}, u32[]{:S(2)}) collective-permute-start(f32[128,512]{0,1:T(8,128)S(1)} %bitcast.88), channel_id=1, source_target_pairs={{32,0},{64,32},{96,64},{128,96},{160,128},{192,160},{224,192},{33,... | collective-permute-start | bytes 786440 | tf_op jit(solution)/shard_map/ppermute | solution.py:18
  69.7 2.2 copy-start.3
  76.5 2.0 copy-start.1
  79.8 22.5 %collective-permute-start.4 = (f32[2048,128]{0,1:T(8,128)}, f32[2048,128]{0,1:T(8,128)S(1)}, u32[]{:S(2)}, u32[]{:S(2)}) collective-permute-start(f32[2048,128]{0,1:T(8,128)} %get-tuple-element.15), channel_id=1, source_target_pairs={{0,1},{1,2},{2,3},{3,4},{4,5},{5,6},{6,7},{7,8},{8,9},{9,10},{10,1... | collective-permute-start | bytes 3145736 | tf_op jit(solution)/shard_map/ppermute | solution.py:17
  85.6 24.6 %collective-permute-start.5 = (f32[2048,128]{0,1:T(8,128)S(1)}, f32[2048,128]{0,1:T(8,128)S(1)}, u32[]{:S(2)}, u32[]{:S(2)}) collective-permute-start(f32[2048,128]{0,1:T(8,128)S(1)} %get-tuple-element.16), channel_id=1, source_target_pairs={{1,0},{2,1},{3,2},{4,3},{5,4},{6,5},{7,6},{8,7},{9,8},{10,9},{11,1... | collective-permute-start | bytes 3145736 | tf_op jit(solution)/shard_map/ppermute | solution.py:18
  116.7 2.0 copy-start.2
  120.0 14.0 %collective-permute-start.6 = (f32[2048,128]{0,1:T(8,128)}, f32[2048,128]{0,1:T(8,128)S(1)}, u32[]{:S(2)}, u32[]{:S(2)}) collective-permute-start(f32[2048,128]{0,1:T(8,128)} %get-tuple-element.13), channel_id=1, source_target_pairs={{0,1},{1,2},{2,3},{3,4},{4,5},{5,6},{6,7},{7,8},{8,9},{9,10},{10,1... | collective-permute-start | bytes 3145736 | tf_op jit(solution)/shard_map/ppermute | solution.py:17
  121.9 30.0 %collective-permute-start.7 = (f32[2048,128]{0,1:T(8,128)S(1)}, f32[2048,128]{0,1:T(8,128)S(1)}, u32[]{:S(2)}, u32[]{:S(2)}) collective-permute-start(f32[2048,128]{0,1:T(8,128)S(1)} %get-tuple-element.14), channel_id=1, source_target_pairs={{1,0},{2,1},{3,2},{4,3},{5,4},{6,5},{7,6},{8,7},{9,8},{10,9},{11,1... | collective-permute-start | bytes 3145736 | tf_op jit(solution)/shard_map/ppermute | solution.py:18
  159.8 5.3 copy-start.5
  171.3 356.9 %all-reduce.13.cloned.1.call-start = ((), (), s32[]{:S(2)}) async-start(), calls=%async_computation | async-start | bytes 4194304 | tf_op jit(solution)/shard_map/psum | solution.py:93
Sparse Core Ops, SparseCore 0:
  171.4 108.9 all-gather.2
Sparse Core Ops, SparseCore 1:
  179.3 348.8 all-reduce.12
